TPU v7x, 256 devices: a whole 4x4x8 slice. The times are simulated.
256 devices in a mesh: floor: 8 (over x, core), facade: 32 (over z, y).
Axes of the slice: x: 4, y: 4, z: 8, core: 2. Of those that a mesh axis runs over, the one named last changes fastest.
Arguments:
- interface_rhs: float32 [8, 32, 2, 256, 128], P('floor', 'facade'), may hold values from -40 to 40
- inverse_factor: float32 [8, 32, 1024, 1024], P('floor', 'facade')
- near_coupling: bfloat16 [8, 32, 1024, 1024], P('floor', 'facade'), may hold values from -0.09375 to 0.09375
- near_pattern: int32 [8, 32, 8, 8], P('floor', 'facade'), may hold values from 0 to 1, as said below
Outputs:
- multipliers: float32 [8, 32, 2, 256, 128], P('floor', 'facade')
- residual: float32 [8, 32, 2, 256, 128], P('floor', 'facade')
Inputs may be any that keep to these rules, and one draw needn't show every extreme that they name: `near_pattern`: every diagonal block is set; each subdomain has from 8 to 32 blocks set, and in every draw some subdomain has exactly 32.
All inputs are finite; a program needn't handle non-finite values.
Results may differ from a plain program's by a relative error of at most 0.0022.
Values sent between devices are 32-bit elements; how exact they have to be, the bound alone decides.
A program may use at most 64 MiB of HBM per device.

v0:
```python
import jax
import jax.numpy as jnp
from jax import lax
from jax.sharding import PartitionSpec as P

ITERS = 4
finest = lax.Precision.HIGHEST


def shifted(value, axis, steps):
    count = lax.axis_size(axis)
    first, last = (max(0, -steps), min(count, count - steps))
    return lax.ppermute(value, axis, [(source, source + steps) for source in range(first, last)])


def from_behind(value, axis, steps):
    count = lax.axis_size(axis)
    pairs = [(source, (source + steps) % count) for source in range(count)]
    return lax.ppermute(value, axis, pairs)


def owned_inner(left_side, right_side):
    return jnp.sum(left_side * right_side, axis=(0, 1))


def local(interface_rhs, inverse_factor, near_coupling, near_pattern):
    factor = inverse_factor[0, 0]
    coupling = near_coupling[0, 0]
    pattern = near_pattern[0, 0]
    faces = interface_rhs.shape[3]
    cases = interface_rhs.shape[4]
    width_all = 4 * faces
    blocks = pattern.shape[0]
    block_rows = width_all // blocks
    floor_pos = lax.axis_index("floor")
    floors = lax.axis_size("floor")
    top_keep = (floor_pos < floors - 1).astype(jnp.float32)
    expanded = jnp.repeat(jnp.repeat(pattern, block_rows, axis=0), block_rows, axis=1).astype(
        jnp.bfloat16
    )
    masked = coupling * expanded
    rhs_owned = jnp.stack([interface_rhs[0, 0, 0] * top_keep, interface_rhs[0, 0, 1]])
    multipliers = jnp.zeros_like(rhs_owned)
    residual = rhs_owned

    def norm_of(vector):
        return lax.psum(owned_inner(vector, vector), ("floor", "facade"))

    direction = rhs_owned
    norm_now = norm_of(residual)
    for sweep in range(ITERS):
        below = shifted(direction[0], "floor", 1)
        beside = from_behind(direction[1], "facade", 1)
        apply_flat = jnp.stack([-below, direction[0], -beside, direction[1]]).reshape(
            width_all, cases
        )
        inner = jnp.dot(factor, apply_flat, precision=finest, preferred_element_type=jnp.float32)
        outer = jnp.einsum(
            "ji,jr->ir", factor, inner, precision=finest, preferred_element_type=jnp.float32
        )
        rounded = apply_flat.astype(jnp.bfloat16)
        forward = jnp.dot(masked, rounded, preferred_element_type=jnp.float32).astype(jnp.bfloat16)
        image = (
            outer + jnp.einsum("ji,jr->ir", masked, forward, preferred_element_type=jnp.float32)
        ).reshape(4, faces, cases)
        above = shifted(image[0], "floor", -1)
        beyond = from_behind(image[2], "facade", -1)
        image = jnp.stack([(image[1] - above) * top_keep, image[3] - beyond])
        step_size = norm_now / lax.psum(owned_inner(direction, image), ("floor", "facade"))
        multipliers = multipliers + step_size * direction
        residual = residual - step_size * image
        if sweep + 1 < ITERS:
            norm_next = norm_of(residual)
            direction = residual + norm_next / norm_now * direction
            norm_now = norm_next
    return (multipliers[None, None], residual[None, None])


def solution(mesh):
    placed = (
        P("floor", "facade", None, None, None),
        P("floor", "facade", None, None),
        P("floor", "facade", None, None),
        P("floor", "facade", None, None),
    )
    return jax.shard_map(
        local,
        mesh=mesh,
        in_specs=placed,
        out_specs=(P("floor", "facade", None, None, None), P("floor", "facade", None, None, None)),
        check_vma=False,
    )
```

profile of v0, /device:TPU:1, one launch (start us, length us, event | category | flops | bytes accessed | tf_op | source)
XLA Modules:
  0.0 693.5 jit_solution(7314364137194731607)
XLA Ops:
  1.8 4.5 collective-permute-start
  21.3 6.7 fusion.14
  31.1 4.6 fusion.27
  37.6 4.4 collective-permute-done.2
  42.7 7.2 %collective-permute-start.3 = (f32[256,128]{0,1:T(8,128)S(1)}, f32[256,128]{0,1:T(8,128)S(1)}, u32[]{:S(2)}, u32[]{:S(2)}) collective-permute-start(f32[256,128]{0,1:T(8,128)S(1)} %get-tuple-element.40), channel_id=1, source_target_pairs={{0,31},{1,0},{2,1},{3,2},{4,3},{5,4},{6,5},{7,6},{8,7},{9,8},{10,9... | collective-permute-start | bytes 393224 | tf_op jit(solution)/shard_map/ppermute | solution.py:19
  52.6 77.5 %all-reduce = (f32[128]{0:T(128)S(1)}, f32[128]{0:T(128)S(1)}) all-reduce(f32[128]{0:T(128)S(1)} %get-tuple-element.7, f32[128]{0:T(128)S(1)} %get-tuple-element.6), channel_id=1, replica_groups=mesh['floor'=8,'facade'=32] {'floor','facade'}, use_global_device_ids=true, to_apply=%region_1.0 | all-reduce | flops 256 | bytes 2048 | tf_op jit(solution)/shard_map/psum | solution.py:47
  130.3 73.4 %psum.58 = f32[128]{0:T(128)S(1)} all-reduce(f32[128]{0:T(128)S(1)} %multiply_reduce_fusion.4), channel_id=1, replica_groups=mesh['floor'=8,'facade'=32] {'floor','facade'}, use_global_device_ids=true, to_apply=%region_5.0 | all-reduce | flops 128 | bytes 1024 | tf_op jit(solution)/shard_map/psum | solution.py:47
  207.1 4.5 collective-permute-done.5
  213.7 7.5 %fusion.10 = f32[128,1024]{1,0:T(8,128)} fusion(f32[1024,128]{1,0:T(8,128)S(1)} %bitcast.183, f32[1,1,1024,1024]{3,2,1,0:T(8,128)} %param.5), kind=kOutput, calls=%fused_computation.10 | convolution fusion | flops 1610612736 | bytes 5242880 | tf_op jit(solution)/shard_map/dot_general | solution.py:57
  222.0 3.9 fusion.67
  225.9 4.7 fusion.33
  240.4 78.1 %psum.59 = f32[128]{0:T(128)S(1)} all-reduce(f32[128]{0:T(128)S(1)} %multiply_reduce_fusion.3), channel_id=1, replica_groups=mesh['floor'=8,'facade'=32] {'floor','facade'}, use_global_device_ids=true, to_apply=%region_7.0 | all-reduce | flops 128 | bytes 1024 | tf_op jit(solution)/shard_map/psum | solution.py:69
  318.8 72.4 %psum.60 = f32[128]{0:T(128)S(1)} all-reduce(f32[128]{0:T(128)S(1)} %get-tuple-element.10), channel_id=1, replica_groups=mesh['floor'=8,'facade'=32] {'floor','facade'}, use_global_device_ids=true, to_apply=%region_9.0 | all-reduce | flops 128 | bytes 1024 | tf_op jit(solution)/shard_map/psum | solution.py:47
  394.3 4.8 collective-permute-done.9
  402.1 7.6 %fusion.6 = f32[128,1024]{1,0:T(8,128)} fusion(f32[1024,128]{1,0:T(8,128)} %bitcast.184, f32[1,1,1024,1024]{3,2,1,0:T(8,128)} %param.5), kind=kOutput, calls=%fused_computation.6 | convolution fusion | flops 1610612736 | bytes 5242880 | tf_op jit(solution)/shard_map/dot_general | solution.py:57
  409.9 3.8 fusion.64
  413.7 4.9 fusion.39
  428.2 77.6 %psum.61 = f32[128]{0:T(128)S(1)} all-reduce(f32[128]{0:T(128)S(1)} %multiply_reduce_fusion.1), channel_id=1, replica_groups=mesh['floor'=8,'facade'=32] {'floor','facade'}, use_global_device_ids=true, to_apply=%region_11.0 | all-reduce | flops 128 | bytes 1024 | tf_op jit(solution)/shard_map/psum | solution.py:69
  506.1 72.6 %psum.62 = f32[128]{0:T(128)S(1)} all-reduce(f32[128]{0:T(128)S(1)} %multiply_reduce_fusion), channel_id=1, replica_groups=mesh['floor'=8,'facade'=32] {'floor','facade'}, use_global_device_ids=true, to_apply=%region_13.0 | all-reduce | flops 128 | bytes 1024 | tf_op jit(solution)/shard_map/psum | solution.py:47
  582.3 4.8 collective-permute-done.13
  588.2 6.7 fusion.2
  599.7 4.6 fusion.45
  604.5 3.6 collective-permute-start.14
  613.5 77.6 %psum.63 = f32[128]{0:T(128)S(1)} all-reduce(f32[128]{0:T(128)S(1)} %fusion.74), channel_id=1, replica_groups=mesh['floor'=8,'facade'=32] {'floor','facade'}, use_global_device_ids=true, to_apply=%region_15.0 | all-reduce | flops 128 | bytes 1024 | tf_op jit(solution)/shard_map/psum | solution.py:69
  (132 shorter events, 74.0 us)
Async XLA Ops:
  1.8 18.4 %collective-permute-start = (f32[256,128]{0,1:T(8,128)S(1)}, f32[256,128]{0,1:T(8,128)S(1)}, u32[]{:S(2)}, u32[]{:S(2)}) collective-permute-start(f32[256,128]{0,1:T(8,128)S(1)} %fusion.121), channel_id=1, source_target_pairs={{0,32},{32,64},{64,96},{96,128},{128,160},{160,192},{192,224},{1,3... | collective-permute-start | bytes 393224 | tf_op jit(solution)/shard_map/ppermute | solution.py:13
  6.4 13.8 %collective-permute-start.1 = (f32[256,128]{0,1:T(8,128)S(1)}, f32[256,128]{0,1:T(8,128)S(1)}, u32[]{:S(2)}, u32[]{:S(2)}) collective-permute-start(f32[256,128]{0,1:T(8,128)S(1)} %bitcast.173), channel_id=1, source_target_pairs={{0,1},{1,2},{2,3},{3,4},{4,5},{5,6},{6,7},{7,8},{8,9},{9,10},{10,1... | collective-permute-start | bytes 393224 | tf_op jit(solution)/shard_map/ppermute | solution.py:19
  35.7 6.3 collective-permute-start.2
  42.7 9.1 %collective-permute-start.3 = (f32[256,128]{0,1:T(8,128)S(1)}, f32[256,128]{0,1:T(8,128)S(1)}, u32[]{:S(2)}, u32[]{:S(2)}) collective-permute-start(f32[256,128]{0,1:T(8,128)S(1)} %get-tuple-element.40), channel_id=1, source_target_pairs={{0,31},{1,0},{2,1},{3,2},{4,3},{5,4},{6,5},{7,6},{8,7},{9,8},{10,9... | collective-permute-start | bytes 393224 | tf_op jit(solution)/shard_map/ppermute | solution.py:19
  203.8 7.8 %collective-permute-start.5 = (f32[256,128]{0,1:T(8,128)S(1)}, f32[256,128]{0,1:T(8,128)S(1)}, u32[]{:S(2)}, u32[]{:S(2)}) collective-permute-start(f32[256,128]{0,1:T(8,128)S(1)} %get-tuple-element.50), channel_id=1, source_target_pairs={{0,1},{1,2},{2,3},{3,4},{4,5},{5,6},{6,7},{7,8},{8,9},{9,10},{10,1... | collective-permute-start | bytes 393224 | tf_op jit(solution)/shard_map/ppermute | solution.py:19
  204.5 7.1 %collective-permute-start.4 = (f32[256,128]{0,1:T(8,128)S(1)}, f32[256,128]{0,1:T(8,128)S(1)}, u32[]{:S(2)}, u32[]{:S(2)}) collective-permute-start(f32[256,128]{0,1:T(8,128)S(1)} %get-tuple-element.49), channel_id=1, source_target_pairs={{0,32},{32,64},{64,96},{96,128},{128,160},{160,192},{192,224},{1,3... | collective-permute-start | bytes 393224 | tf_op jit(solution)/shard_map/ppermute | solution.py:13
  230.7 7.0 %collective-permute-start.6 = (f32[256,128]{0,1:T(8,128)S(1)}, f32[256,128]{0,1:T(8,128)S(1)}, u32[]{:S(2)}, u32[]{:S(2)}) collective-permute-start(f32[256,128]{0,1:T(8,128)S(1)} %get-tuple-element.38), channel_id=1, source_target_pairs={{32,0},{64,32},{96,64},{128,96},{160,128},{192,160},{224,192},{33,... | collective-permute-start | bytes 393224 | tf_op jit(solution)/shard_map/ppermute | solution.py:13
  234.2 5.3 collective-permute-start.7
  391.3 7.8 %collective-permute-start.9 = (f32[256,128]{0,1:T(8,128)S(1)}, f32[256,128]{0,1:T(8,128)S(1)}, u32[]{:S(2)}, u32[]{:S(2)}) collective-permute-start(f32[256,128]{0,1:T(8,128)S(1)} %get-tuple-element.46), channel_id=1, source_target_pairs={{0,1},{1,2},{2,3},{3,4},{4,5},{5,6},{6,7},{7,8},{8,9},{9,10},{10,1... | collective-permute-start | bytes 393224 | tf_op jit(solution)/shard_map/ppermute | solution.py:19
  391.7 7.4 %collective-permute-start.8 = (f32[256,128]{0,1:T(8,128)S(1)}, f32[256,128]{0,1:T(8,128)S(1)}, u32[]{:S(2)}, u32[]{:S(2)}) collective-permute-start(f32[256,128]{0,1:T(8,128)S(1)} %get-tuple-element.45), channel_id=1, source_target_pairs={{0,32},{32,64},{64,96},{96,128},{128,160},{160,192},{192,224},{1,3... | collective-permute-start | bytes 393224 | tf_op jit(solution)/shard_map/ppermute | solution.py:13
  418.6 6.6 collective-permute-start.10
  422.1 5.3 collective-permute-start.11
  579.4 7.8 %collective-permute-start.13 = (f32[256,128]{0,1:T(8,128)S(1)}, f32[256,128]{0,1:T(8,128)S(1)}, u32[]{:S(2)}, u32[]{:S(2)}) collective-permute-start(f32[256,128]{0,1:T(8,128)S(1)} %get-tuple-element.42), channel_id=1, source_target_pairs={{0,1},{1,2},{2,3},{3,4},{4,5},{5,6},{6,7},{7,8},{8,9},{9,10},{10,1... | collective-permute-start | bytes 393224 | tf_op jit(solution)/shard_map/ppermute | solution.py:19
  579.8 7.4 %collective-permute-start.12 = (f32[256,128]{0,1:T(8,128)S(1)}, f32[256,128]{0,1:T(8,128)S(1)}, u32[]{:S(2)}, u32[]{:S(2)}) collective-permute-start(f32[256,128]{0,1:T(8,128)S(1)} %get-tuple-element.41), channel_id=1, source_target_pairs={{0,32},{32,64},{64,96},{96,128},{128,160},{160,192},{192,224},{1,3... | collective-permute-start | bytes 393224 | tf_op jit(solution)/shard_map/ppermute | solution.py:13
  604.4 86.8 %copy-start.17 = (f32[128]{0:T(128)S(1)}, f32[128]{0:T(128)}, u32[]{:S(2)}) copy-start(f32[128]{0:T(128)} %copy-done.16) | copy-start | bytes 1540
  604.4 86.8 %copy-start.6 = (f32[1,1,1,256,128]{3,4,2,1,0:T(8,128)S(1)}, f32[1,1,1,256,128]{3,4,2,1,0:T(8,128)}, u32[]{:S(2)}) copy-start(f32[1,1,1,256,128]{3,4,2,1,0:T(8,128)} %get-tuple-element.25) | copy-start | bytes 393220
  604.4 86.8 %copy-start.7 = (f32[1,1,1,256,128]{3,4,2,1,0:T(8,128)S(1)}, f32[1,1,1,256,128]{3,4,2,1,0:T(8,128)}, u32[]{:S(2)}) copy-start(f32[1,1,1,256,128]{3,4,2,1,0:T(8,128)} %get-tuple-element.27) | copy-start | bytes 393220
  604.4 86.8 %copy-start.8 = (f32[1,1,1,256,128]{3,4,2,1,0:T(8,128)S(1)}, f32[1,1,1,256,128]{3,4,2,1,0:T(8,128)}, u32[]{:S(2)}) copy-start(f32[1,1,1,256,128]{3,4,2,1,0:T(8,128)} %get-tuple-element.16) | copy-start | bytes 393220
  604.4 86.8 %copy-start.9 = (f32[1,1,1,256,128]{3,4,2,1,0:T(8,128)S(1)}, f32[1,1,1,256,128]{3,4,2,1,0:T(8,128)}, u32[]{:S(2)}) copy-start(f32[1,1,1,256,128]{3,4,2,1,0:T(8,128)} %get-tuple-element.31) | copy-start | bytes 393220
  604.4 86.8 %copy-start.10 = (f32[1,1,1,256,128]{3,4,2,1,0:T(8,128)S(1)}, f32[1,1,1,256,128]{3,4,2,1,0:T(8,128)}, u32[]{:S(2)}) copy-start(f32[1,1,1,256,128]{3,4,2,1,0:T(8,128)} %get-tuple-element.20) | copy-start | bytes 393220
  604.4 86.8 %copy-start.11 = (f32[1,1,1,256,128]{3,4,2,1,0:T(8,128)S(1)}, f32[1,1,1,256,128]{3,4,2,1,0:T(8,128)}, u32[]{:S(2)}) copy-start(f32[1,1,1,256,128]{3,4,2,1,0:T(8,128)} %get-tuple-element.33) | copy-start | bytes 393220
  604.4 86.8 %copy-start.13 = (f32[128]{0:T(128)S(1)}, f32[128]{0:T(128)}, u32[]{:S(2)}) copy-start(f32[128]{0:T(128)} %copy-done.12) | copy-start | bytes 1540
  604.5 6.8 collective-permute-start.14
  608.1 5.3 collective-permute-start.15
  (10 other events, 143.8 us)
where the time goes:
time: 703 us; the launch traced here: 694 us
  blocking collectives  529 us (75%)
  matrix products  61.1 us (9%)
  starting transfers between devices  36.9 us (5%)
  waiting for transfers between devices  34 us (5%)
  local copies, waits for them, and re-layouts  17.6 us (3%)
  other arithmetic  13.2 us (2%)
    psum x4, blocking collectives, norm_of(): return lax.psum(owned_inner(vector, vector), ('floor', 'facade'))  296 us
    psum x3, blocking collectives, local(): lax.psum(owned_inner(direction, image), ('floor', 'facade'))  233 us
    dot_general x4, matrix products, local(): jnp.dot(factor, apply_flat, precision=finest, preferred_element_type=jnp....  28.4 us
    ppermute x8, starting transfers between devices, shifted(): lax.ppermute(value, axis, [(source, source + steps) for source in range(f...  24.6 us
    ppermute x8, waiting for transfers between devices, from_behind(): return lax.ppermute(value, axis, pairs)  22.1 us
    dot_general x4, matrix products, local(): jnp.einsum('ji,jr->ir', factor, inner, precision=finest, preferred_elemen...  18.8 us
  transfers between devices with their start and end apart: 16, of which 11 were waited for; matrix products, arithmetic and copies ran while one was open for 2% of the time, Pallas kernels for 0%

commit v1 on v0

--- a/solution.py
+++ b/solution.py
@@ -66,7 +66,7 @@
         above = shifted(image[0], "floor", -1)
         beyond = from_behind(image[2], "facade", -1)
         image = jnp.stack([(image[1] - above) * top_keep, image[3] - beyond])
-        step_size = norm_now / lax.psum(owned_inner(direction, image), ("floor", "facade"))
+        step_size = norm_now / lax.psum(lax.psum(owned_inner(direction, image), "facade"), "floor")
         multipliers = multipliers + step_size * direction
         residual = residual - step_size * image
         if sweep + 1 < ITERS:

time: 703 us -> 814 us (1.16)
  blocking collectives: 529 us -> 640 us
    psum x3 -> x8, blocking collectives: 233 us -> 348 us  [the longest x4 237 us: local(): lax.psum(owned_inner(direction, image), 'facade')]
  transfers between devices with their start and end apart: 16 -> 16, of which waited for: 11 -> 11; matrix products, arithmetic and copies ran while one was open for 2% -> 1% of each run, Pallas kernels for 0% -> 0%
where the time goes in v1:
time: 814 us; the launch traced here: 805 us
  blocking collectives  640 us (79%)
  matrix products  61.1 us (8%)
  starting transfers between devices  36.6 us (4%)
  waiting for transfers between devices  34.5 us (4%)
  local copies, waits for them, and re-layouts  17.7 us (2%)
  other arithmetic  13.2 us (2%)
    psum x4, blocking collectives, norm_of(): return lax.psum(owned_inner(vector, vector), ('floor', 'facade'))  292 us
    psum x4, blocking collectives, local(): lax.psum(owned_inner(direction, image), 'facade')  237 us
    psum x4, blocking collectives, local(): lax.psum(lax.psum(owned_inner(direction, image), 'facade'), 'floor')  111 us
    dot_general x4, matrix products, local(): jnp.dot(factor, apply_flat, precision=finest, preferred_element_type=jnp....  28.5 us
    ppermute x8, starting transfers between devices, shifted(): lax.ppermute(value, axis, [(source, source + steps) for source in range(f...  25.9 us
    ppermute x8, waiting for transfers between devices, from_behind(): return lax.ppermute(value, axis, pairs)  23.3 us
    dot_general x4, matrix products, local(): jnp.einsum('ji,jr->ir', factor, inner, precision=finest, preferred_elemen...  18.8 us
  transfers between devices with their start and end apart: 16, of which 11 were waited for; matrix products, arithmetic and copies ran while one was open for 1% of the time, Pallas kernels for 0%

profile of v1, /device:TPU:1, one launch (start us, length us, event | category | flops | bytes accessed | tf_op | source)
XLA Modules:
  0.0 804.5 jit_solution(6842077314537690020)
XLA Ops:
  1.8 4.5 collective-permute-start
  21.4 6.7 fusion.14
  31.1 4.6 fusion.27
  42.7 7.2 collective-permute-start.3
  52.7 60.9 %psum.85 = f32[128]{0:T(128)S(1)} all-reduce(f32[128]{0:T(128)S(1)} %get-tuple-element.6), channel_id=1, replica_groups=mesh['floor'=8,'facade'=32] {'facade'}, use_global_device_ids=true, to_apply=%region_3.0 | all-reduce | flops 128 | bytes 1024 | tf_op jit(solution)/shard_map/psum | solution.py:69
  113.6 25.8 %psum.86 = f32[128]{0:T(128)S(1)} all-reduce(f32[128]{0:T(128)S(1)} %psum.85), channel_id=1, replica_groups=mesh['floor'=8,'facade'=32] {'floor'}, use_global_device_ids=true, to_apply=%region_4.0 | all-reduce | flops 128 | bytes 1024 | tf_op jit(solution)/shard_map/psum | solution.py:69
  139.3 72.8 %psum.84 = f32[128]{0:T(128)S(1)} all-reduce(f32[128]{0:T(128)S(1)} %get-tuple-element.7), channel_id=1, replica_groups=mesh['floor'=8,'facade'=32] {'floor','facade'}, use_global_device_ids=true, to_apply=%region_1.0 | all-reduce | flops 128 | bytes 1024 | tf_op jit(solution)/shard_map/psum | solution.py:47
  212.4 73.7 %psum.87 = f32[128]{0:T(128)S(1)} all-reduce(f32[128]{0:T(128)S(1)} %multiply_reduce_fusion.4), channel_id=1, replica_groups=mesh['floor'=8,'facade'=32] {'floor','facade'}, use_global_device_ids=true, to_apply=%region_6.0 | all-reduce | flops 128 | bytes 1024 | tf_op jit(solution)/shard_map/psum | solution.py:47
  289.5 4.6 collective-permute-done.5
  296.2 7.5 fusion.10
  308.4 4.7 fusion.33
  322.9 58.9 %psum.88 = f32[128]{0:T(128)S(1)} all-reduce(f32[128]{0:T(128)S(1)} %multiply_reduce_fusion.3), channel_id=1, replica_groups=mesh['floor'=8,'facade'=32] {'facade'}, use_global_device_ids=true, to_apply=%region_8.0 | all-reduce | flops 128 | bytes 1024 | tf_op jit(solution)/shard_map/psum | solution.py:69
  381.8 28.8 %psum.89 = f32[128]{0:T(128)S(1)} all-reduce(f32[128]{0:T(128)S(1)} %psum.88), channel_id=1, replica_groups=mesh['floor'=8,'facade'=32] {'floor'}, use_global_device_ids=true, to_apply=%region_9.0 | all-reduce | flops 128 | bytes 1024 | tf_op jit(solution)/shard_map/psum | solution.py:69
  410.8 72.9 %psum.90 = f32[128]{0:T(128)S(1)} all-reduce(f32[128]{0:T(128)S(1)} %get-tuple-element.8), channel_id=1, replica_groups=mesh['floor'=8,'facade'=32] {'floor','facade'}, use_global_device_ids=true, to_apply=%region_11.0 | all-reduce | flops 128 | bytes 1024 | tf_op jit(solution)/shard_map/psum | solution.py:47
  486.6 4.5 collective-permute-done.9
  494.1 7.6 fusion.6
  505.7 4.9 fusion.39
  520.8 58.7 %psum.91 = f32[128]{0:T(128)S(1)} all-reduce(f32[128]{0:T(128)S(1)} %multiply_reduce_fusion.1), channel_id=1, replica_groups=mesh['floor'=8,'facade'=32] {'facade'}, use_global_device_ids=true, to_apply=%region_13.0 | all-reduce | flops 128 | bytes 1024 | tf_op jit(solution)/shard_map/psum | solution.py:69
  579.5 28.1 %psum.92 = f32[128]{0:T(128)S(1)} all-reduce(f32[128]{0:T(128)S(1)} %psum.91), channel_id=1, replica_groups=mesh['floor'=8,'facade'=32] {'floor'}, use_global_device_ids=true, to_apply=%region_14.0 | all-reduce | flops 128 | bytes 1024 | tf_op jit(solution)/shard_map/psum | solution.py:69
  607.7 72.7 %psum.93 = f32[128]{0:T(128)S(1)} all-reduce(f32[128]{0:T(128)S(1)} %multiply_reduce_fusion), channel_id=1, replica_groups=mesh['floor'=8,'facade'=32] {'floor','facade'}, use_global_device_ids=true, to_apply=%region_16.0 | all-reduce | flops 128 | bytes 1024 | tf_op jit(solution)/shard_map/psum | solution.py:47
  689.6 6.7 fusion.2
  701.1 4.6 fusion.45
  715.4 58.7 %psum.94 = f32[128]{0:T(128)S(1)} all-reduce(f32[128]{0:T(128)S(1)} %fusion.74), channel_id=1, replica_groups=mesh['floor'=8,'facade'=32] {'facade'}, use_global_device_ids=true, to_apply=%region_18.0 | all-reduce | flops 128 | bytes 1024 | tf_op jit(solution)/shard_map/psum | solution.py:69
  774.1 28.1 %psum.95 = f32[128]{0:T(128)S(1)} all-reduce(f32[128]{0:T(128)S(1)} %psum.94), channel_id=1, replica_groups=mesh['floor'=8,'facade'=32] {'floor'}, use_global_device_ids=true, to_apply=%region_19.0 | all-reduce | flops 128 | bytes 1024 | tf_op jit(solution)/shard_map/psum | solution.py:69
  (137 shorter events, 95.1 us)
Async XLA Ops:
  1.8 18.5 %collective-permute-start = (f32[256,128]{0,1:T(8,128)S(1)}, f32[256,128]{0,1:T(8,128)S(1)}, u32[]{:S(2)}, u32[]{:S(2)}) collective-permute-start(f32[256,128]{0,1:T(8,128)S(1)} %fusion.121), channel_id=1, source_target_pairs={{0,32},{32,64},{64,96},{96,128},{128,160},{160,192},{192,224},{1,3... | collective-permute-start | bytes 393224 | tf_op jit(solution)/shard_map/ppermute | solution.py:13
  6.4 13.9 %collective-permute-start.1 = (f32[256,128]{0,1:T(8,128)S(1)}, f32[256,128]{0,1:T(8,128)S(1)}, u32[]{:S(2)}, u32[]{:S(2)}) collective-permute-start(f32[256,128]{0,1:T(8,128)S(1)} %bitcast.173), channel_id=1, source_target_pairs={{0,1},{1,2},{2,3},{3,4},{4,5},{5,6},{6,7},{7,8},{8,9},{9,10},{10,1... | collective-permute-start | bytes 393224 | tf_op jit(solution)/shard_map/ppermute | solution.py:19
  35.8 6.3 collective-permute-start.2
  42.7 9.1 %collective-permute-start.3 = (f32[256,128]{0,1:T(8,128)S(1)}, f32[256,128]{0,1:T(8,128)S(1)}, u32[]{:S(2)}, u32[]{:S(2)}) collective-permute-start(f32[256,128]{0,1:T(8,128)S(1)} %get-tuple-element.38), channel_id=1, source_target_pairs={{0,31},{1,0},{2,1},{3,2},{4,3},{5,4},{6,5},{7,6},{8,7},{9,8},{10,9... | collective-permute-start | bytes 393224 | tf_op jit(solution)/shard_map/ppermute | solution.py:19
  286.3 7.8 collective-permute-start.5
  286.9 7.1 collective-permute-start.4
  313.2 6.9 collective-permute-start.6
  316.6 5.3 collective-permute-start.7
  483.9 7.2 collective-permute-start.9
  484.0 7.1 collective-permute-start.8
  510.6 6.3 collective-permute-start.10
  514.7 5.3 collective-permute-start.11
  681.1 7.4 collective-permute-start.13
  681.4 7.1 collective-permute-start.12
  705.7 96.4 %copy-start.17 = (f32[128]{0:T(128)S(1)}, f32[128]{0:T(128)}, u32[]{:S(2)}) copy-start(f32[128]{0:T(128)} %copy-done.16) | copy-start | bytes 1540
  705.7 96.4 %copy-start.6 = (f32[1,1,1,256,128]{3,4,2,1,0:T(8,128)S(1)}, f32[1,1,1,256,128]{3,4,2,1,0:T(8,128)}, u32[]{:S(2)}) copy-start(f32[1,1,1,256,128]{3,4,2,1,0:T(8,128)} %get-tuple-element.23) | copy-start | bytes 393220
  705.7 96.4 %copy-start.7 = (f32[1,1,1,256,128]{3,4,2,1,0:T(8,128)S(1)}, f32[1,1,1,256,128]{3,4,2,1,0:T(8,128)}, u32[]{:S(2)}) copy-start(f32[1,1,1,256,128]{3,4,2,1,0:T(8,128)} %get-tuple-element.25) | copy-start | bytes 393220
  705.7 96.4 %copy-start.8 = (f32[1,1,1,256,128]{3,4,2,1,0:T(8,128)S(1)}, f32[1,1,1,256,128]{3,4,2,1,0:T(8,128)}, u32[]{:S(2)}) copy-start(f32[1,1,1,256,128]{3,4,2,1,0:T(8,128)} %get-tuple-element.14) | copy-start | bytes 393220
  705.8 96.4 %copy-start.9 = (f32[1,1,1,256,128]{3,4,2,1,0:T(8,128)S(1)}, f32[1,1,1,256,128]{3,4,2,1,0:T(8,128)}, u32[]{:S(2)}) copy-start(f32[1,1,1,256,128]{3,4,2,1,0:T(8,128)} %get-tuple-element.29) | copy-start | bytes 393220
  705.8 96.4 %copy-start.10 = (f32[1,1,1,256,128]{3,4,2,1,0:T(8,128)S(1)}, f32[1,1,1,256,128]{3,4,2,1,0:T(8,128)}, u32[]{:S(2)}) copy-start(f32[1,1,1,256,128]{3,4,2,1,0:T(8,128)} %get-tuple-element.18) | copy-start | bytes 393220
  705.8 96.4 %copy-start.11 = (f32[1,1,1,256,128]{3,4,2,1,0:T(8,128)S(1)}, f32[1,1,1,256,128]{3,4,2,1,0:T(8,128)}, u32[]{:S(2)}) copy-start(f32[1,1,1,256,128]{3,4,2,1,0:T(8,128)} %get-tuple-element.31) | copy-start | bytes 393220
  705.8 96.4 %copy-start.13 = (f32[128]{0:T(128)S(1)}, f32[128]{0:T(128)}, u32[]{:S(2)}) copy-start(f32[128]{0:T(128)} %copy-done.12) | copy-start | bytes 1540
  705.8 6.4 collective-permute-start.14
  710.0 5.3 collective-permute-start.15
  (10 other events, 152.5 us)
